TPU v7x, 32 devices: a whole 2x2x4 slice. The times are simulated.
32 devices in a mesh: prow: 8 (over z, x), pcol: 4 (over y, core).
Axes of the slice: x: 2, y: 2, z: 4, core: 2. Of those that a mesh axis runs over, the one named last changes fastest.
Arguments:
- sigma_top: bfloat16 [8, 8, 128, 128], P('prow', 'pcol'), may hold values from -6 to 6
- factor_one: bfloat16 [8, 8, 128, 128], P('prow', 'pcol'), may hold values from -0.1875 to 0.1875
- inverse_one: bfloat16 [8, 128, 128], P('prow'), may hold values from -0.5 to 0.5
- pattern_one: int32 [8, 8], replicated, may hold values from 0 to 7, as said below
- factor_two: bfloat16 [8, 8, 128, 128], P('prow', 'pcol'), may hold values from -0.25 to 0.25
- parent_block: bfloat16 [8, 128, 128], P('prow'), may hold values from -0.25 to 0.25
- inverse_two: bfloat16 [8, 128, 128], P('prow'), may hold values from -0.5 to 0.5
- parent_two: int32 [8], replicated, may hold values from 0 to 7
- keep_two: int32 [8, 8], replicated, may hold values 0 or 1
Outputs:
- inverse_top_one: bfloat16 [8, 8, 128, 128], P('prow')
- diag_one: float32 [8, 128, 128], P('prow')
- inverse_top_two: bfloat16 [8, 8, 128, 128], P('prow')
- inverse_parent_two: float32 [8, 128, 128], P('prow')
- diag_two: float32 [8, 128, 128], P('prow')
Inputs may be any that keep to these rules, and one draw needn't show every extreme that they name: Each row of pattern_one lists 8 distinct block rows of the top region. keep_two[i, k] = 1 where level-two supernode i's pattern holds the k-th tile of its parent's pattern. parent_two names level-one supernodes.
All inputs are finite; a program needn't handle non-finite values.
Results may differ from a plain program's by a relative error of at most 0.023.
Values may be sent and summed in bfloat16 or wider, within the bound.
A program may use at most 64 MiB of HBM per device.

v0:
```python
import jax
import jax.numpy as jnp
from jax import lax
from jax.sharding import PartitionSpec as P

highest = lax.Precision.HIGHEST


def split_product(form, left, right):
    upper_part = right.astype(jnp.bfloat16)
    lower_part = (right - upper_part.astype(jnp.float32)).astype(jnp.bfloat16)
    first = jnp.einsum(form, left, upper_part, preferred_element_type=jnp.float32)
    return first + jnp.einsum(form, left, lower_part, preferred_element_type=jnp.float32)


def body(
    sigma_top,
    factor_one,
    inverse_one,
    pattern_one,
    factor_two,
    parent_block,
    inverse_two,
    parent_two,
    keep_two,
):
    rows_here = sigma_top.shape[0]
    cols_here = sigma_top.shape[1]
    tile_width = sigma_top.shape[2]
    prow_index = lax.axis_index("prow")
    pcol_index = lax.axis_index("pcol")
    first_row = prow_index * rows_here
    column_ids = pcol_index * cols_here + jnp.arange(cols_here, dtype=jnp.int32)
    top_rows = first_row + jnp.arange(rows_here, dtype=jnp.int32)
    owner_column = first_row // cols_here
    diagonal_owner = owner_column == pcol_index
    offset = jnp.clip(first_row - pcol_index * cols_here, 0, cols_here - rows_here)
    total_one = pattern_one.shape[0]
    local_one = factor_one.shape[0]
    lower_one = jnp.tril(inverse_one)
    scaled_local = jnp.einsum(
        "jkwv,jvx->jkwx", factor_one, lower_one, preferred_element_type=jnp.float32
    ).astype(jnp.bfloat16)
    scaled_rows = lax.all_gather(scaled_local, "pcol", axis=1, tiled=True)
    own_pattern = lax.dynamic_slice_in_dim(pattern_one, prow_index * local_one, local_one, 0)
    picker_one = (own_pattern[:, :, None] == column_ids[None, None, :]).astype(jnp.bfloat16)
    spread_one = jnp.einsum(
        "jkc,jkwv->jcwv", picker_one, scaled_rows, preferred_element_type=jnp.float32
    ).astype(jnp.bfloat16)
    spread_all = lax.all_gather(spread_one, "prow", axis=0, tiled=True)
    partial_one = jnp.einsum(
        "acwv,jcvx->ajwx", sigma_top, spread_all, preferred_element_type=jnp.float32
    )
    summed_one = lax.psum(partial_one.astype(jnp.bfloat16), "pcol").astype(jnp.float32)
    member_one = jnp.sum(
        (pattern_one[None, :, :] == top_rows[:, None, None]).astype(jnp.float32), axis=2
    )
    inverse_top_one = (-summed_one * member_one[:, :, None, None]).astype(jnp.bfloat16)
    own_rows = lax.dynamic_slice_in_dim(spread_all, offset, rows_here, 1)
    quadratic_one = split_product("jawv,ajwx->jvx", own_rows, summed_one)
    quadratic_one = jnp.where(diagonal_owner, quadratic_one, 0.0)
    lower_float = lower_one.astype(jnp.float32)
    gram_one = jnp.einsum("jwv,jwx->jvx", lower_float, lower_float, precision=highest)
    placed = lax.dynamic_update_slice_in_dim(
        jnp.zeros((total_one, tile_width, tile_width), jnp.float32),
        gram_one,
        prow_index * local_one,
        0,
    )
    partial_diag = quadratic_one + jnp.where(pcol_index == 0, placed, 0.0)
    diagonal_all = lax.psum(partial_diag, ("prow", "pcol"))
    diag_one = lax.dynamic_slice_in_dim(diagonal_all, prow_index * local_one, local_one, 0)
    local_two = factor_two.shape[0]
    lower_two = jnp.tril(inverse_two)
    scaled_two = jnp.einsum(
        "ikwv,ivx->ikwx", factor_two, lower_two, preferred_element_type=jnp.float32
    ).astype(jnp.bfloat16)
    scaled_parent = jnp.einsum(
        "iwv,ivx->iwx", parent_block, lower_two, preferred_element_type=jnp.float32
    ).astype(jnp.bfloat16)
    scaled_rows_two = lax.all_gather(scaled_two, "pcol", axis=1, tiled=True)
    parent_hot = (parent_two[:, None] == jnp.arange(total_one, dtype=jnp.int32)[None, :]).astype(
        jnp.int32
    )
    parent_pattern = jnp.sum(parent_hot[:, :, None] * pattern_one[None, :, :], axis=1)
    own_parent_pattern = lax.dynamic_slice_in_dim(
        parent_pattern, prow_index * local_two, local_two, 0
    )
    own_keep = lax.dynamic_slice_in_dim(keep_two, prow_index * local_two, local_two, 0)
    picker_two = (
        (own_parent_pattern[:, :, None] == column_ids[None, None, :]).astype(jnp.int32)
        * own_keep[:, :, None]
    ).astype(jnp.bfloat16)
    spread_two = jnp.einsum(
        "ikc,ikwv->icwv", picker_two, scaled_rows_two, preferred_element_type=jnp.float32
    ).astype(jnp.bfloat16)
    spread_all_two, parent_all = (
        lax.all_gather(spread_two, "prow", axis=0, tiled=True),
        lax.all_gather(scaled_parent, "prow", axis=0, tiled=True),
    )
    partial_two = jnp.einsum(
        "acwv,icvx->aiwx", sigma_top, spread_all_two, preferred_element_type=jnp.float32
    )
    inherited = jnp.einsum(
        "ij,ajwv->aiwv",
        parent_hot.astype(jnp.bfloat16),
        inverse_top_one,
        preferred_element_type=jnp.float32,
    ).astype(jnp.bfloat16)
    carried_rows = jnp.einsum(
        "aiwv,ivx->aiwx", inherited, parent_all, preferred_element_type=jnp.float32
    )
    partial_two = partial_two + jnp.where(diagonal_owner, carried_rows, 0.0)
    summed_two = lax.psum(partial_two.astype(jnp.bfloat16), "pcol").astype(jnp.float32)
    member_two = jnp.sum(
        (parent_pattern[None, :, :] == top_rows[:, None, None]).astype(jnp.float32)
        * keep_two[None, :, :].astype(jnp.float32),
        axis=2,
    )
    inverse_top_two = (-summed_two * member_two[:, :, None, None]).astype(jnp.bfloat16)
    own_two = lax.dynamic_slice_in_dim(spread_all_two, offset, rows_here, 1)
    cross = jnp.einsum("aiwv,iawx->ivx", inherited, own_two, preferred_element_type=jnp.float32)
    quadratic_two = split_product("iawv,aiwx->ivx", own_two, summed_two)
    cross = jnp.where(diagonal_owner, cross, 0.0)
    quadratic_two = jnp.where(diagonal_owner, quadratic_two, 0.0)
    cross_part, quadratic_part = (
        lax.psum_scatter(
            cross.astype(jnp.bfloat16), "prow", scatter_dimension=0, tiled=True
        ).astype(jnp.float32),
        lax.psum_scatter(
            quadratic_two.astype(jnp.bfloat16), "prow", scatter_dimension=0, tiled=True
        ).astype(jnp.float32),
    )
    cross_sum, quadratic_sum = (
        lax.psum(cross_part.astype(jnp.bfloat16), "pcol").astype(jnp.float32),
        lax.psum(quadratic_part.astype(jnp.bfloat16), "pcol").astype(jnp.float32),
    )
    own_hot = lax.dynamic_slice_in_dim(parent_hot, prow_index * local_two, local_two, 0).astype(
        jnp.float32
    )
    parent_diag = jnp.einsum("ij,jwv->iwv", own_hot, diagonal_all, precision=highest)
    parent_float = scaled_parent.astype(jnp.float32)
    carried = cross_sum + jnp.einsum("iwv,ivx->iwx", parent_diag, parent_float, precision=highest)
    lower_two_float = lower_two.astype(jnp.float32)
    diag_two = jnp.einsum("iwv,iwx->ivx", lower_two_float, lower_two_float, precision=highest)
    diag_two = (
        diag_two
        + quadratic_sum
        + jnp.einsum("iwv,iwx->ivx", parent_float, carried, precision=highest)
    )
    return (inverse_top_one, diag_one, inverse_top_two, -carried, diag_two)


def solution(mesh):
    in_specs = (
        P("prow", "pcol", None, None),
        P("prow", "pcol", None, None),
        P("prow", None, None),
        P(),
        P("prow", "pcol", None, None),
        P("prow", None, None),
        P("prow", None, None),
        P(),
        P(),
    )
    out_specs = (
        P("prow", None, None, None),
        P("prow", None, None),
        P("prow", None, None, None),
        P("prow", None, None),
        P("prow", None, None),
    )
    return jax.shard_map(body, mesh=mesh, in_specs=in_specs, out_specs=out_specs, check_vma=False)
```

profile of v0, /device:TPU:0, one launch (start us, length us, event | category | flops | bytes accessed | tf_op | source)
XLA Modules:
  0.0 453.0 jit_solution(8151209483114322396)
XLA Ops:
  7.2 1.1 fusion.10
  8.4 7.2 %all-gather = bf16[8,128,128]{2,1,0:T(8,128)(2,1)S(1)} all-gather(bf16[2,128,128]{2,1,0:T(8,128)(2,1)S(1)} %copy.72), channel_id=2, replica_groups=mesh['prow'=8,'pcol'=4] {'pcol'}, dimensions={0}, use_global_device_ids=true | all-gather | bytes 327680 | tf_op jit(solution)/shard_map/all_gather | solution.py:44
  16.0 31.9 %all-gather.1 = bf16[16,128,128]{2,1,0:T(8,128)(2,1)S(1)} all-gather(bf16[2,128,128]{2,1,0:T(8,128)(2,1)S(1)} %copy.74), channel_id=3, replica_groups=mesh['prow'=8,'pcol'=4] {'prow'}, dimensions={0}, use_global_device_ids=true | all-gather | bytes 589824 | tf_op jit(solution)/shard_map/all_gather | solution.py:50
  47.9 1.1 fusion.7
  50.9 5.8 %all-gather.2 = bf16[8,128,128]{2,1,0:T(8,128)(2,1)S(1)} all-gather(bf16[2,128,128]{2,1,0:T(8,128)(2,1)S(1)} %copy.79), channel_id=4, replica_groups=mesh['prow'=8,'pcol'=4] {'pcol'}, dimensions={0}, use_global_device_ids=true | all-gather | bytes 327680 | tf_op jit(solution)/shard_map/all_gather | solution.py:81
  57.0 31.5 %all-gather.3 = bf16[16,128,128]{2,1,0:T(8,128)(2,1)S(1)} all-gather(bf16[2,128,128]{2,1,0:T(8,128)(2,1)S(1)} %copy.81), channel_id=5, replica_groups=mesh['prow'=8,'pcol'=4] {'prow'}, dimensions={0}, use_global_device_ids=true | all-gather | bytes 589824 | tf_op jit(solution)/shard_map/all_gather | solution.py:98
  88.7 26.4 %all-gather.4 = bf16[1024,128]{0,1:T(8,128)(2,1)S(1)} all-gather(bf16[128,128]{0,1:T(8,128)(2,1)S(1)} %bitcast.162), channel_id=6, replica_groups=mesh['prow'=8,'pcol'=4] {'prow'}, dimensions={0}, use_global_device_ids=true | all-gather | bytes 294912 | tf_op jit(solution)/shard_map/all_gather | solution.py:99
  115.5 1.1 fusion.112
  117.2 0.9 fusion.9
  118.2 0.9 copy-done.1
  121.5 1.0 fusion.6
  122.7 26.8 %all-reduce.10.cloned.1.call-done = bf16[1,8,128,128]{2,3,1,0:T(8,128)(2,1)} async-done(((bf16[1,8,128,128]{2,3,1,0:T(8,128)(2,1)}), bf16[1,8,128,128]{2,3,1,0:T(8,128)(2,1)}) %all-reduce.10.cloned.1.call-update) | async-done | bytes 262160 | tf_op jit(solution)/shard_map/psum | solution.py:114
  149.5 1.3 fusion.32
  150.9 1.0 fusion.3
  152.1 0.9 copy.92
  153.0 0.9 copy.93
  153.9 128.7 %all-reduce.8.cloned.1.call-done = f32[8,128,128]{2,1,0:T(8,128)} async-done(((f32[8,128,128]{2,1,0:T(8,128)}), f32[8,128,128]{2,1,0:T(8,128)}) %all-reduce.8.cloned.1.call-update) | async-done | bytes 524304 | tf_op jit(solution)/shard_map/psum | solution.py:71
  282.6 1.8 fusion.24
  284.5 61.9 %reduce-scatter.3.cloned.1.call-done = bf16[1,128,128]{2,1,0:T(8,128)(2,1)} async-done(((bf16[8,128,128]{2,1,0:T(8,128)(2,1)}), bf16[1,128,128]{2,1,0:T(8,128)(2,1)}) %reduce-scatter.3.cloned.1.call-update) | async-done | bytes 32784 | tf_op jit(solution)/shard_map/reduce_scatter | solution.py:127
  346.4 63.8 %reduce-scatter.5.cloned.1.call-done = bf16[1,128,128]{2,1,0:T(8,128)(2,1)} async-done(((bf16[8,128,128]{2,1,0:T(8,128)(2,1)}), bf16[1,128,128]{2,1,0:T(8,128)(2,1)}) %reduce-scatter.5.cloned.1.call-update) | async-done | bytes 32784 | tf_op jit(solution)/shard_map/reduce_scatter | solution.py:130
  410.3 1.5 constant_dynamic-slice_fusion.3
  411.8 31.2 %all-reduce.12.cloned.1.call-done = (bf16[1,128,128]{2,1,0:T(8,128)(2,1)}, bf16[1,128,128]{2,1,0:T(8,128)(2,1)}) async-done(((bf16[1,128,128]{2,1,0:T(8,128)(2,1)}, bf16[1,128,128]{2,1,0:T(8,128)(2,1)}), (bf16[1,128,128]{2,1,0:T(8,128)(2,1)}, bf16[1,128,128]{2,1,0:T(8,128)(2,1)})) %all-reduce.12.cloned.1.call-update) | async-done | bytes 65552 | tf_op jit(solution)/shard_map/psum | solution.py:135
  442.9 1.6 fusion.102
  445.3 0.8 fusion.15
  (64 shorter events, 7.6 us)
Async XLA Ops:
  7.2 40.7 %copy-start = (bf16[1,2,128,128]{3,2,1,0:T(8,128)(2,1)S(1)}, bf16[1,2,128,128]{3,2,1,0:T(8,128)(2,1)}, u32[]{:S(2)}) copy-start(bf16[1,2,128,128]{3,2,1,0:T(8,128)(2,1)} %param.9) | copy-start | bytes 196612
  7.2 108.3 %all-reduce.6.cloned.1.call-start = ((), (), s32[]{:S(2)}) async-start(), calls=%async_computation.2 | async-start | bytes 524288 | tf_op jit(solution)/shard_map/psum | solution.py:54
  8.4 7.2 %copy-start.9 = (s32[8,8]{1,0:T(8,128)S(1)}, s32[8,8]{1,0:T(8,128)}, u32[]{:S(2)}) copy-start(s32[8,8]{1,0:T(8,128)} %param.12) | copy-start | bytes 772
  48.9 100.6 %all-reduce.10.cloned.1.call-start = ((), (), s32[]{:S(2)}) async-start(), calls=%async_computation.4 | async-start | bytes 524288 | tf_op jit(solution)/shard_map/psum | solution.py:114
  49.1 0.7 copy-start.11
  49.1 1.4 copy-start.6
  49.4 1.1 copy-start.4
  49.8 0.7 copy-start.10
  57.0 31.5 %copy-start.7 = (bf16[1,128,128]{2,1,0:T(8,128)(2,1)S(1)}, bf16[1,128,128]{2,1,0:T(8,128)(2,1)}, u32[]{:S(2)}) copy-start(bf16[1,128,128]{2,1,0:T(8,128)(2,1)} %param.14) | copy-start | bytes 98308
  118.2 0.9 copy-start.1
  118.2 164.4 %all-reduce.8.cloned.1.call-start = ((), (), s32[]{:S(2)}) async-start(), calls=%async_computation.3 | async-start | bytes 1048576 | tf_op jit(solution)/shard_map/psum | solution.py:71
  119.4 0.8 copy-start.5
  120.4 0.8 copy-start.2
  121.2 225.2 %reduce-scatter.3.cloned.1.call-start = ((), (), s32[]{:S(2)}) async-start(), calls=%async_computation.5 | async-start | bytes 294912 | tf_op jit(solution)/shard_map/reduce_scatter | solution.py:127
  122.6 287.7 %reduce-scatter.5.cloned.1.call-start = ((), (), s32[]{:S(2)}) async-start(), calls=%async_computation.6 | async-start | bytes 294912 | tf_op jit(solution)/shard_map/reduce_scatter | solution.py:130
  149.5 1.3 copy-start.3
  151.9 291.0 %all-reduce.12.cloned.1.call-start = ((), (), s32[]{:S(2)}) async-start(), calls=%async_computation.7 | async-start | bytes 131072 | tf_op jit(solution)/shard_map/psum | solution.py:135
  444.5 0.8 copy-start.8
Sparse Core Ops, SparseCore 0:
  49.1 32.7 all-reduce.5
  118.3 31.1 all-reduce.9
  154.8 127.7 all-reduce.7
  286.2 60.2 reduce-scatter.2
  350.0 60.2 reduce-scatter.4
  412.6 30.2 all-reduce.11
where the time goes:
time: 454 us; the launch traced here: 453 us
  waiting for transfers between devices  313 us (69%)
  blocking collectives  103 us (23%)
  between operations  14.4 us (3%)
  matrix products  13.2 us (3%)
  local copies, waits for them, and re-layouts  8.08 us (2%)
    psum x1, waiting for transfers between devices, body(): diagonal_all = lax.psum(partial_diag, ('prow', 'pcol'))  129 us
    reduce_scatter x1, waiting for transfers between devices, body(): lax.psum_scatter(quadratic_two.astype(jnp.bfloat16), 'prow', scatter_dime...  63.8 us
    reduce_scatter x1, waiting for transfers between devices, body(): lax.psum_scatter(cross.astype(jnp.bfloat16), 'prow', scatter_dimension=0,...  61.9 us
    all_gather x1, blocking collectives, body(): spread_all = lax.all_gather(spread_one, 'prow', axis=0, tiled=True)  31.9 us
    all_gather x1, blocking collectives, body(): lax.all_gather(spread_two, 'prow', axis=0, tiled=True)  31.5 us
    psum x1, waiting for transfers between devices, body(): lax.psum(cross_part.astype(jnp.bfloat16), 'pcol').astype(jnp.float32)  31.2 us
    psum x1, waiting for transfers between devices, body(): lax.psum(partial_two.astype(jnp.bfloat16), 'pcol').astype(jnp.float32)  26.8 us
    all_gather x1, blocking collectives, body(): lax.all_gather(scaled_parent, 'prow', axis=0, tiled=True)  26.4 us
  transfers between devices with their start and end apart: 6, of which 5 were waited for; matrix products, arithmetic and copies ran while one was open for 3% of the time, Pallas kernels for 0%

commit v1 on v0

--- a/solution.py
+++ b/solution.py
@@ -68,7 +68,7 @@
         0,
     )
     partial_diag = quadratic_one + jnp.where(pcol_index == 0, placed, 0.0)
-    diagonal_all = lax.psum(partial_diag, ("prow", "pcol"))
+    diagonal_all = lax.psum(lax.psum(partial_diag, "pcol"), "prow")
     diag_one = lax.dynamic_slice_in_dim(diagonal_all, prow_index * local_one, local_one, 0)
     local_two = factor_two.shape[0]
     lower_two = jnp.tril(inverse_two)

time: 454 us -> 433 us (0.954)
  waiting for transfers between devices: 313 us -> 292 us
    psum x1 -> x2, waiting for transfers between devices: 129 us -> 108 us  [body(): diagonal_all = lax.psum(lax.psum(partial_diag, 'pcol'), 'prow')]
  transfers between devices with their start and end apart: 6 -> 7, of which waited for: 5 -> 6; matrix products, arithmetic and copies ran while one was open for 3% -> 2% of each run, Pallas kernels for 0% -> 0%
where the time goes in v1:
time: 433 us; the launch traced here: 432 us
  waiting for transfers between devices  292 us (67%)
  blocking collectives  103 us (24%)
  between operations  14.4 us (3%)
  matrix products  13.2 us (3%)
  local copies, waits for them, and re-layouts  8.07 us (2%)
    psum x2, waiting for transfers between devices, body(): diagonal_all = lax.psum(lax.psum(partial_diag, 'pcol'), 'prow')  108 us
    reduce_scatter x1, waiting for transfers between devices, body(): lax.psum_scatter(quadratic_two.astype(jnp.bfloat16), 'prow', scatter_dime...  63.5 us
    reduce_scatter x1, waiting for transfers between devices, body(): lax.psum_scatter(cross.astype(jnp.bfloat16), 'prow', scatter_dimension=0,...  62.3 us
    all_gather x1, blocking collectives, body(): spread_all = lax.all_gather(spread_one, 'prow', axis=0, tiled=True)  31.9 us
    all_gather x1, blocking collectives, body(): lax.all_gather(spread_two, 'prow', axis=0, tiled=True)  31.5 us
    psum x1, waiting for transfers between devices, body(): lax.psum(cross_part.astype(jnp.bfloat16), 'pcol').astype(jnp.float32)  31.1 us
    psum x1, waiting for transfers between devices, body(): lax.psum(partial_two.astype(jnp.bfloat16), 'pcol').astype(jnp.float32)  26.9 us
    all_gather x1, blocking collectives, body(): lax.all_gather(scaled_parent, 'prow', axis=0, tiled=True)  26.4 us
  transfers between devices with their start and end apart: 7, of which 6 were waited for; matrix products, arithmetic and copies ran while one was open for 2% of the time, Pallas kernels for 0%

profile of v1, /device:TPU:0, one launch (start us, length us, event | category | flops | bytes accessed | tf_op | source)
XLA Modules:
  0.0 432.2 jit_solution(14513007944716377772)
XLA Ops:
  7.2 1.1 fusion.10
  8.4 7.2 %all-gather = bf16[8,128,128]{2,1,0:T(8,128)(2,1)S(1)} all-gather(bf16[2,128,128]{2,1,0:T(8,128)(2,1)S(1)} %copy.72), channel_id=2, replica_groups=mesh['prow'=8,'pcol'=4] {'pcol'}, dimensions={0}, use_global_device_ids=true | all-gather | bytes 327680 | tf_op jit(solution)/shard_map/all_gather | solution.py:44
  16.0 31.9 %all-gather.1 = bf16[16,128,128]{2,1,0:T(8,128)(2,1)S(1)} all-gather(bf16[2,128,128]{2,1,0:T(8,128)(2,1)S(1)} %copy.74), channel_id=3, replica_groups=mesh['prow'=8,'pcol'=4] {'prow'}, dimensions={0}, use_global_device_ids=true | all-gather | bytes 589824 | tf_op jit(solution)/shard_map/all_gather | solution.py:50
  47.9 1.1 fusion.7
  50.9 5.8 %all-gather.2 = bf16[8,128,128]{2,1,0:T(8,128)(2,1)S(1)} all-gather(bf16[2,128,128]{2,1,0:T(8,128)(2,1)S(1)} %copy.79), channel_id=4, replica_groups=mesh['prow'=8,'pcol'=4] {'pcol'}, dimensions={0}, use_global_device_ids=true | all-gather | bytes 327680 | tf_op jit(solution)/shard_map/all_gather | solution.py:81
  57.0 31.5 %all-gather.3 = bf16[16,128,128]{2,1,0:T(8,128)(2,1)S(1)} all-gather(bf16[2,128,128]{2,1,0:T(8,128)(2,1)S(1)} %copy.81), channel_id=5, replica_groups=mesh['prow'=8,'pcol'=4] {'prow'}, dimensions={0}, use_global_device_ids=true | all-gather | bytes 589824 | tf_op jit(solution)/shard_map/all_gather | solution.py:98
  88.7 26.4 %all-gather.4 = bf16[1024,128]{0,1:T(8,128)(2,1)S(1)} all-gather(bf16[128,128]{0,1:T(8,128)(2,1)S(1)} %bitcast.162), channel_id=6, replica_groups=mesh['prow'=8,'pcol'=4] {'prow'}, dimensions={0}, use_global_device_ids=true | all-gather | bytes 294912 | tf_op jit(solution)/shard_map/all_gather | solution.py:99
  115.5 1.1 fusion.112
  117.2 0.9 fusion.9
  118.2 0.9 copy-done.1
  121.5 1.0 fusion.6
  122.6 26.9 %all-reduce.13.cloned.1.call-done = bf16[1,8,128,128]{2,3,1,0:T(8,128)(2,1)} async-done(((bf16[1,8,128,128]{2,3,1,0:T(8,128)(2,1)}), bf16[1,8,128,128]{2,3,1,0:T(8,128)(2,1)}) %all-reduce.13.cloned.1.call-update) | async-done | bytes 262160 | tf_op jit(solution)/shard_map/psum | solution.py:114
  149.5 1.3 fusion.32
  150.9 1.0 fusion.3
  152.0 33.2 %all-reduce.9.cloned.1.call-done = f32[8,128,128]{2,1,0:T(8,128)} async-done(((f32[8,128,128]{2,1,0:T(8,128)}), f32[8,128,128]{2,1,0:T(8,128)}) %all-reduce.9.cloned.1.call-update) | async-done | bytes 524304 | tf_op jit(solution)/shard_map/psum | solution.py:71
  185.4 0.9 copy.92
  186.4 0.9 copy.93
  187.2 62.3 %reduce-scatter.3.cloned.1.call-done = bf16[1,128,128]{2,1,0:T(8,128)(2,1)} async-done(((bf16[8,128,128]{2,1,0:T(8,128)(2,1)}), bf16[1,128,128]{2,1,0:T(8,128)(2,1)}) %reduce-scatter.3.cloned.1.call-update) | async-done | bytes 32784 | tf_op jit(solution)/shard_map/reduce_scatter | solution.py:127
  249.5 63.5 %reduce-scatter.5.cloned.1.call-done = bf16[1,128,128]{2,1,0:T(8,128)(2,1)} async-done(((bf16[8,128,128]{2,1,0:T(8,128)(2,1)}), bf16[1,128,128]{2,1,0:T(8,128)(2,1)}) %reduce-scatter.5.cloned.1.call-update) | async-done | bytes 32784 | tf_op jit(solution)/shard_map/reduce_scatter | solution.py:130
  313.1 74.6 %all-reduce.11.cloned.1.call-done = f32[8,128,128]{2,1,0:T(8,128)} async-done(((f32[8,128,128]{2,1,0:T(8,128)}), f32[8,128,128]{2,1,0:T(8,128)}) %all-reduce.11.cloned.1.call-update) | async-done | bytes 524304 | tf_op jit(solution)/shard_map/psum | solution.py:71
  387.7 1.8 fusion.24
  389.5 31.1 %all-reduce.15.cloned.1.call-done = (bf16[1,128,128]{2,1,0:T(8,128)(2,1)}, bf16[1,128,128]{2,1,0:T(8,128)(2,1)}) async-done(((bf16[1,128,128]{2,1,0:T(8,128)(2,1)}, bf16[1,128,128]{2,1,0:T(8,128)(2,1)}), (bf16[1,128,128]{2,1,0:T(8,128)(2,1)}, bf16[1,128,128]{2,1,0:T(8,128)(2,1)})) %all-reduce.15.cloned.1.call-update) | async-done | bytes 65552 | tf_op jit(solution)/shard_map/psum | solution.py:135
  420.7 1.6 fusion.102
  423.9 1.5 constant_dynamic-slice_fusion.3
  (67 shorter events, 8.4 us)
Async XLA Ops:
  7.2 40.7 %copy-start = (bf16[1,2,128,128]{3,2,1,0:T(8,128)(2,1)S(1)}, bf16[1,2,128,128]{3,2,1,0:T(8,128)(2,1)}, u32[]{:S(2)}) copy-start(bf16[1,2,128,128]{3,2,1,0:T(8,128)(2,1)} %param.9) | copy-start | bytes 196612
  7.2 108.3 %all-reduce.7.cloned.1.call-start = ((), (), s32[]{:S(2)}) async-start(), calls=%async_computation.2 | async-start | bytes 524288 | tf_op jit(solution)/shard_map/psum | solution.py:54
  8.4 7.2 %copy-start.9 = (s32[8,8]{1,0:T(8,128)S(1)}, s32[8,8]{1,0:T(8,128)}, u32[]{:S(2)}) copy-start(s32[8,8]{1,0:T(8,128)} %param.12) | copy-start | bytes 772
  48.9 100.6 %all-reduce.13.cloned.1.call-start = ((), (), s32[]{:S(2)}) async-start(), calls=%async_computation.5 | async-start | bytes 524288 | tf_op jit(solution)/shard_map/psum | solution.py:114
  49.1 0.7 copy-start.11
  49.1 1.4 copy-start.6
  49.4 1.1 copy-start.4
  49.8 0.7 copy-start.10
  57.0 31.5 %copy-start.7 = (bf16[1,128,128]{2,1,0:T(8,128)(2,1)S(1)}, bf16[1,128,128]{2,1,0:T(8,128)(2,1)}, u32[]{:S(2)}) copy-start(bf16[1,128,128]{2,1,0:T(8,128)(2,1)} %param.14) | copy-start | bytes 98308
  118.2 0.9 copy-start.1
  118.2 66.9 %all-reduce.9.cloned.1.call-start = ((), (), s32[]{:S(2)}) async-start(), calls=%async_computation.3 | async-start | bytes 1048576 | tf_op jit(solution)/shard_map/psum | solution.py:71
  119.4 0.8 copy-start.5
  120.4 0.8 copy-start.2
  121.2 128.3 %reduce-scatter.3.cloned.1.call-start = ((), (), s32[]{:S(2)}) async-start(), calls=%async_computation.6 | async-start | bytes 294912 | tf_op jit(solution)/shard_map/reduce_scatter | solution.py:127
  122.6 190.4 %reduce-scatter.5.cloned.1.call-start = ((), (), s32[]{:S(2)}) async-start(), calls=%async_computation.7 | async-start | bytes 294912 | tf_op jit(solution)/shard_map/reduce_scatter | solution.py:130
  149.5 1.3 copy-start.3
  151.9 235.8 %all-reduce.11.cloned.1.call-start = ((), (), s32[]{:S(2)}) async-start(), calls=%async_computation.4 | async-start | bytes 1048576 | tf_op jit(solution)/shard_map/psum | solution.py:71
  185.1 235.6 %all-reduce.15.cloned.1.call-start = ((), (), s32[]{:S(2)}) async-start(), calls=%async_computation.8 | async-start | bytes 131072 | tf_op jit(solution)/shard_map/psum | solution.py:135
  422.3 0.8 copy-start.8
Sparse Core Ops, SparseCore 0:
  49.1 32.7 all-reduce.6
  118.3 31.1 all-reduce.12
  151.9 33.1 all-reduce.8
  188.3 61.2 reduce-scatter.2
  252.7 60.2 reduce-scatter.4
  316.3 71.3 all-reduce.10
  390.2 30.4 all-reduce.14
